TPU v7x, 32 devices: a whole 2x2x4 slice. The times are simulated.
32 devices in a mesh: rep: 4 (over z), exp: 8 (over y, x, core).
Axes of the slice: x: 2, y: 2, z: 4, core: 2. Of those that a mesh axis runs over, the one named last changes fastest.
Arguments:
- tokens: bfloat16 [4096, 1024], P(('rep', 'exp')), may hold values from -6 to 6
- expert_ids: int32 [4096, 2], P(('rep', 'exp')), may hold values from 0 to 7, all different within a row; in each aligned block of 128 rows (0 to 127, 128 to 255, ...) at most 64 rows name the same one
- gate_weights: float32 [4096, 2], P(('rep', 'exp')), may hold values from 0.2 to 1
- w_gate: bfloat16 [8, 1408, 1024], P('exp'), may hold values from -0.1875 to 0.1875
- w_up: bfloat16 [8, 1408, 1024], P('exp'), may hold values from -0.1875 to 0.1875
- w_down: bfloat16 [8, 1408, 1024], P('exp'), may hold values from -0.15625 to 0.15625
- grad_out: bfloat16 [4096, 1024], P(('rep', 'exp')), may hold values from -3 to 3
Outputs:
- layer_output: bfloat16 [4096, 1024], P(('rep', 'exp'))
- grad_tokens: bfloat16 [4096, 1024], P(('rep', 'exp'))
- grad_gates: float32 [4096, 2], P(('rep', 'exp'))
- grad_w_gate: bfloat16 [8, 1408, 1024], P('exp', 'rep')
- grad_w_up: bfloat16 [8, 1408, 1024], P('exp', 'rep')
- grad_w_down: bfloat16 [8, 1408, 1024], P('exp', 'rep')
Inputs may be any that keep to these rules, and one draw needn't show every extreme that they name: `expert_ids`: each token names 2 different experts. In each aligned block of 128 tokens (the tokens of one device) no expert is named more than 64 times, a bound that some block reaches.
All inputs are finite; a program needn't handle non-finite values.
Results may differ from a plain program's by a relative error of at most 0.0095.
Values may be sent and summed in bfloat16 or wider, within the bound.
A program may use at most 128 MiB of HBM per device.

v0:
```python
import jax
import jax.numpy as jnp
from jax import lax
from jax.experimental import pallas as pl
from jax.experimental.pallas import tpu as pltpu
from jax.sharding import PartitionSpec as P


def silu_parts(gate_pre):
    sigmoid_value = jax.nn.sigmoid(gate_pre)
    active = gate_pre * sigmoid_value
    slope_term = sigmoid_value * (1.0 + gate_pre * (1.0 - sigmoid_value))
    return (active, slope_term)


def place_pairs(expert_ids, experts, capacity):
    flat_ids = expert_ids.reshape(-1)
    onehot = (flat_ids[:, None] == jnp.arange(experts, dtype=jnp.int32)[None, :]).astype(jnp.int32)
    before = jnp.cumsum(onehot, axis=0) - onehot
    position = jnp.sum(before * onehot, axis=1)
    return flat_ids * capacity + position


def expert_forward(rows_in, w_gate, w_up, w_down):
    gate_pre = jnp.einsum("erd,efd->erf", rows_in, w_gate, preferred_element_type=jnp.float32)
    up_pre = jnp.einsum("erd,efd->erf", rows_in, w_up, preferred_element_type=jnp.float32)
    active, slope_term = silu_parts(gate_pre)
    hidden = (active * up_pre).astype(jnp.bfloat16)
    outputs = jnp.einsum("erf,efd->erd", hidden, w_down, preferred_element_type=jnp.float32).astype(
        jnp.bfloat16
    )
    return (up_pre, active, slope_term, hidden, outputs)


def expert_backward(rows_grad, up_pre, active, slope_term, w_gate, w_up, w_down):
    grad_hidden = jnp.einsum("erd,efd->erf", rows_grad, w_down, preferred_element_type=jnp.float32)
    grad_gate = (grad_hidden * up_pre * slope_term).astype(jnp.bfloat16)
    grad_up = (grad_hidden * active).astype(jnp.bfloat16)
    from_gate = jnp.einsum("erf,efd->erd", grad_gate, w_gate, preferred_element_type=jnp.float32)
    from_up = jnp.einsum("erf,efd->erd", grad_up, w_up, preferred_element_type=jnp.float32)
    grad_rows = (from_gate + from_up).astype(jnp.bfloat16)
    return (grad_gate, grad_up, grad_rows)


def local_general(tokens, expert_ids, gate_weights, w_gate, w_up, w_down, grad_out):
    local_tokens, model_width = tokens.shape
    top_count = expert_ids.shape[1]
    local_experts = w_gate.shape[0]
    peer_count = lax.axis_size("exp")
    replicas = lax.axis_size("rep")
    experts = local_experts * peer_count
    capacity = 2 * top_count * local_tokens // experts
    target = place_pairs(expert_ids, experts, capacity)
    pair_tokens = jnp.repeat(tokens, top_count, axis=0)
    pair_gates = gate_weights.reshape(-1)
    pair_grads = jnp.repeat(grad_out, top_count, axis=0).astype(jnp.float32)
    scaled_grads = (pair_gates[:, None] * pair_grads).astype(jnp.bfloat16)
    blank_rows = jnp.zeros((experts * capacity, model_width), jnp.bfloat16)
    token_buffer = blank_rows.at[target].set(pair_tokens).reshape(experts, capacity, model_width)
    grad_buffer = blank_rows.at[target].set(scaled_grads).reshape(experts, capacity, model_width)
    rows_in = lax.all_to_all(token_buffer, "exp", split_axis=0, concat_axis=1, tiled=True)
    up_pre, active, slope_term, hidden, outputs = expert_forward(rows_in, w_gate, w_up, w_down)
    returned = lax.all_to_all(outputs, "exp", split_axis=1, concat_axis=0, tiled=True)
    rows_grad = lax.all_to_all(grad_buffer, "exp", split_axis=0, concat_axis=1, tiled=True)
    grad_gate, grad_up, grad_rows = expert_backward(
        rows_grad, up_pre, active, slope_term, w_gate, w_up, w_down
    )
    returned_grads = lax.all_to_all(grad_rows, "exp", split_axis=1, concat_axis=0, tiled=True)
    pair_outputs = returned.reshape(experts * capacity, model_width)[target].astype(jnp.float32)
    pair_input_grads = returned_grads.reshape(experts * capacity, model_width)[target].astype(
        jnp.float32
    )
    weighted = (pair_gates[:, None] * pair_outputs).reshape(local_tokens, top_count, model_width)
    layer_output = jnp.sum(weighted, axis=1).astype(jnp.bfloat16)
    grad_gates = jnp.sum(pair_grads * pair_outputs, axis=1).reshape(local_tokens, top_count)
    grad_tokens = jnp.sum(
        pair_input_grads.reshape(local_tokens, top_count, model_width), axis=1
    ).astype(jnp.bfloat16)
    term_gate = jnp.einsum("erf,erd->fed", grad_gate, rows_in, preferred_element_type=jnp.float32)
    term_up = jnp.einsum("erf,erd->fed", grad_up, rows_in, preferred_element_type=jnp.float32)
    term_down = jnp.einsum("erf,erd->fed", hidden, rows_grad, preferred_element_type=jnp.float32)
    summed = lax.psum_scatter(
        jnp.concatenate([term_gate, term_up, term_down], axis=2).astype(jnp.bfloat16),
        "rep",
        scatter_dimension=0,
        tiled=True,
    ).astype(jnp.float32)
    summed = jnp.swapaxes(summed, 0, 1) / replicas
    grad_w_gate = summed[:, :, :model_width].astype(jnp.bfloat16)
    grad_w_up = summed[:, :, model_width : 2 * model_width].astype(jnp.bfloat16)
    grad_w_down = summed[:, :, 2 * model_width :].astype(jnp.bfloat16)
    return (layer_output, grad_tokens, grad_gates, grad_w_gate, grad_w_up, grad_w_down)


MESH = pl.DeviceIdType.MESH
REPS = 4
PEERS = 8
EXTRA = 16


def dot(a, b, b_dim):
    return lax.dot_general(a, b, (((1,), (b_dim,)), ((), ())), preferred_element_type=jnp.float32)


def moe_kernel(
    tokens_ref, grads_ref, gate_rows_ref, target_ref, gates_ref, w_gate_hbm, w_up_hbm, w_down_hbm,
    out_ref, grad_tokens_ref, grad_gates_ref, dw_gate_ref, dw_up_ref, dw_down_ref,
    all_ref, w_gate, w_up, w_down, rows_in, rows_grad, place_ref, gate_ref, out_acc, grad_acc, leaving, returned,
    acc_gate, acc_up, acc_down,
    load_sem, weight_sem, keep_sem, send_sem, recv_sem, zup_sem, zdown_sem, zrecv_sem, back_send, back_recv,
):
    z = lax.axis_index("rep")
    e = lax.axis_index("exp")
    core, x, y = e % 2, (e // 2) % 2, e // 4
    sib, xn, yn = e + 1 - 2 * core, e + 2 - 4 * x, e + 4 - 8 * y
    diag = xn + yn - e
    count, width = tokens_ref.shape
    rows = all_ref.shape[2]
    capacity = leaving.shape[2]
    share = w_gate.shape[0] // REPS
    first, second = pl.ds(0, rows // 32 * 16), pl.ds(rows // 32 * 16, rows - rows // 32 * 16)

    side = z // 2
    near = z + side * (3 - 2 * z)
    layers = [z]
    for step in range(1, REPS):
        mirrored = step - near if step == 1 else step
        layers.append(mirrored + side * (3 - 2 * mirrored))

    mine = all_ref.at[z, e]
    loads = [
        pltpu.make_async_copy(tokens_ref, all_ref.at[z, e, pl.ds(0, count)], load_sem.at[0]),
        pltpu.make_async_copy(grads_ref, all_ref.at[z, e, pl.ds(count, count)], load_sem.at[1]),
        pltpu.make_async_copy(gate_rows_ref, all_ref.at[z, e, pl.ds(2 * count, EXTRA)], load_sem.at[2]),
    ]
    weights = [
        pltpu.make_async_copy(w_gate_hbm, w_gate, weight_sem.at[0]),
        pltpu.make_async_copy(w_up_hbm, w_up, weight_sem.at[1]),
        pltpu.make_async_copy(w_down_hbm, w_down, weight_sem.at[2]),
    ]
    for copy in loads:
        copy.start()
    for copy in weights:
        copy.start()

    barrier = pltpu.get_barrier_semaphore()
    for shift in range(1, PEERS):
        peer = (e + shift) % PEERS
        pl.semaphore_signal(barrier, inc=1, device_id={"rep": z, "exp": peer}, device_id_type=MESH)

    @pl.when(z > 0)
    def _():
        pl.semaphore_signal(barrier, inc=1, device_id={"rep": z - 1, "exp": e}, device_id_type=MESH)

    @pl.when(z < REPS - 1)
    def _():
        pl.semaphore_signal(barrier, inc=1, device_id={"rep": z + 1, "exp": e}, device_id_type=MESH)

    inside = jnp.logical_and(z > 0, z < REPS - 1)

    @pl.when(inside)
    def _():
        pl.semaphore_wait(barrier, PEERS + 1)

    @pl.when(jnp.logical_not(inside))
    def _():
        pl.semaphore_wait(barrier, PEERS)

    def plane(kind, layer, owner, part, peer):
        block = all_ref.at[layer, owner] if part is None else all_ref.at[layer, owner, part]
        return pltpu.make_async_remote_copy(
            src_ref=block,
            dst_ref=block,
            send_sem=send_sem.at[kind, layer],
            recv_sem=recv_sem.at[kind, layer],
            device_id={"rep": z, "exp": peer},
            device_id_type=MESH,
        )

    def along(sem, layer, step):
        return pltpu.make_async_remote_copy(
            src_ref=all_ref.at[layer, e],
            dst_ref=all_ref.at[layer, e],
            send_sem=sem.at[layer],
            recv_sem=zrecv_sem.at[layer],
            device_id={"rep": z + step, "exp": e},
            device_id_type=MESH,
        )

    def direct(layer):
        return [plane(0, layer, e, None, xn), plane(1, layer, e, None, yn), plane(2, layer, e, None, sib)]

    def relayed(layer):
        return [
            plane(3, layer, xn, first, yn),
            plane(5, layer, xn, None, sib),
            plane(4, layer, yn, second, xn),
            plane(6, layer, yn, None, sib),
        ]

    def pass_on(layer, action):
        @pl.when(jnp.logical_and(layer <= z, z < REPS - 1))
        def _():
            action(along(zup_sem, layer, 1))

        @pl.when(jnp.logical_and(layer >= z, z > 0))
        def _():
            action(along(zdown_sem, layer, -1))

    def inject(step):
        layer = layers[step]
        if step:
            along(zup_sem, layer, 0).wait_recv()
        pass_on(layer, lambda copy: copy.start())
        for copy in direct(layer):
            copy.start()

    def forward(step):
        layer = layers[step]
        copies = relayed(layer)
        plane(0, layer, xn, None, xn).wait_recv()
        copies[0].start()
        copies[1].start()
        plane(1, layer, yn, None, yn).wait_recv()
        copies[2].start()
        copies[3].start()

    def finish(step):
        layer = layers[step]
        plane(3, layer, diag, first, yn).wait_recv()
        plane(4, layer, diag, second, xn).wait_recv()
        plane(7, layer, diag, None, sib).start()

    def arrive(step):
        for kind in (2, 5, 6, 7):
            plane(kind, layers[step], sib, None, sib).wait_recv()

    def drain(step):
        layer = layers[step]
        for copy in direct(layer) + relayed(layer) + [plane(7, layer, diag, None, sib)]:
            copy.wait_send()
        pass_on(layer, lambda copy: copy.wait_send())

    def pick(step):
        layer = layers[step]
        lanes = pl.ds(pl.multiple_of(e * count, count), count)
        for block in range(PEERS):
            parts = all_ref[layer, block, pl.ds(2 * count, EXTRA), lanes].astype(jnp.float32)
            gate_ref[block : block + 1, :] = jnp.sum(parts, axis=0, keepdims=True)
        gates = gate_ref[...]
        used = jnp.where(gates > 0.0, 1.0, 0.0)
        earlier = lax.broadcasted_iota(jnp.int32, (count, count), 0)
        later = lax.broadcasted_iota(jnp.int32, (count, count), 1)
        before = jnp.where(earlier < later, 1.0, 0.0).astype(jnp.bfloat16)
        position = dot(used.astype(jnp.bfloat16), before, 0)
        place_ref[...] = jnp.where(gates > 0.0, position, -1.0)

        def body(block, carry):
            slot = lax.broadcasted_iota(jnp.int32, (capacity, count), 0).astype(jnp.float32)
            select = jnp.where(slot == place_ref[pl.ds(block, 1), :], 1.0, 0.0)
            slot_gates = jnp.sum(select * gate_ref[pl.ds(block, 1), :], axis=1, keepdims=True)
            select = select.astype(jnp.bfloat16)
            span = pl.ds(pl.multiple_of(block * capacity, capacity), capacity)
            rows_in[span, :] = dot(select, all_ref[layer, block, pl.ds(0, count), :], 0).astype(jnp.bfloat16)
            rows_grad[span, :] = (
                slot_gates * dot(select, all_ref[layer, block, pl.ds(count, count), :], 0)
            ).astype(jnp.bfloat16)
            return carry

        lax.fori_loop(0, PEERS, body, 0)

    def pointwise(gate_pre, up_pre, grad_hidden):
        sigmoid = 1.0 / (1.0 + jnp.exp(-gate_pre))
        active = gate_pre * sigmoid
        slope = sigmoid * (1.0 + gate_pre * (1.0 - sigmoid))
        hidden = (active * up_pre).astype(jnp.bfloat16)
        grad_gate = (grad_hidden * up_pre * slope).astype(jnp.bfloat16)
        grad_up = (grad_hidden * active).astype(jnp.bfloat16)
        return hidden, grad_gate, grad_up

    def own_rows(low, high):
        tile = rows_in.shape[0] // 2

        def body(index, carry):
            units = pl.ds(pl.multiple_of((index // 2) * share, share), share)
            span = pl.ds(pl.multiple_of((index % 2) * tile, tile), tile)
            gate, up, down = w_gate[units, :], w_up[units, :], w_down[units, :]
            row_in, row_grad = rows_in[span, :], rows_grad[span, :]
            hidden, grad_gate, grad_up = pointwise(dot(row_in, gate, 1), dot(row_in, up, 1), dot(row_grad, down, 1))
            out_acc[span, :] += dot(hidden, down, 0)
            grad_acc[span, :] += dot(grad_gate, gate, 0) + dot(grad_up, up, 0)
            return carry

        lax.fori_loop(low, high, body, 0)

    def weight_grads(start):
        units = pl.ds(pl.multiple_of(z * share, share), share)
        row_in, row_grad = rows_in[...], rows_grad[...]
        hidden, grad_gate, grad_up = pointwise(
            dot(w_gate[units, :], row_in, 1), dot(w_up[units, :], row_in, 1), dot(w_down[units, :], row_grad, 1)
        )
        for acc, lhs, rhs in ((acc_gate, grad_gate, row_in), (acc_up, grad_up, row_in), (acc_down, hidden, row_grad)):
            if start:
                acc[...] = dot(lhs, rhs, 0)
            else:
                acc[...] += dot(lhs, rhs, 0)

    def back(which, shift, source, slot, peer):
        return pltpu.make_async_remote_copy(
            src_ref=leaving.at[which, source],
            dst_ref=returned.at[which, slot],
            send_sem=back_send.at[which, shift],
            recv_sem=back_recv.at[which, shift],
            device_id={"rep": z, "exp": peer},
            device_id_type=MESH,
        )

    def keep(which):
        return pltpu.make_async_copy(leaving.at[which, e], returned.at[which, e], keep_sem.at[which])

    for copy in loads:
        copy.wait()
    inject(0)
    out_acc[...] = jnp.zeros_like(out_acc)
    grad_acc[...] = jnp.zeros_like(grad_acc)
    for copy in weights:
        copy.wait()
    inject(1)
    forward(0)
    inject(2)
    finish(0)
    forward(1)
    arrive(0)
    pick(0)
    own_rows(0, REPS)
    inject(3)
    finish(1)
    own_rows(REPS, 2 * REPS)
    for which, acc in ((0, out_acc), (1, grad_acc)):
        leaving[which] = acc[...].astype(jnp.bfloat16).reshape(leaving.shape[1:])
    for which in range(2):
        keep(which).start()
        for shift in range(1, PEERS):
            peer = (e + shift) % PEERS
            back(which, shift, peer, e, peer).start()
    forward(2)
    weight_grads(True)
    arrive(1)
    pick(1)
    weight_grads(False)
    finish(2)
    forward(3)
    arrive(2)
    pick(2)
    weight_grads(False)
    for which in range(2):
        keep(which).wait()
        for shift in range(1, PEERS):
            source = (e + PEERS - shift) % PEERS
            back(which, shift, source, source, source).wait_recv()
    outputs = returned[0].reshape(PEERS * capacity, width)
    grads = returned[1].reshape(PEERS * capacity, width)
    column = lax.broadcasted_iota(jnp.int32, (count, PEERS * capacity), 1)
    total = jnp.zeros((count, width), jnp.float32)
    grad_total = jnp.zeros((count, width), jnp.float32)
    cotangent = all_ref[z, e, pl.ds(count, count), :].astype(jnp.float32)
    for choice in range(target_ref.shape[0]):
        place = jnp.where(column == target_ref[choice], 1.0, 0.0).astype(jnp.bfloat16)
        pair = dot(place, outputs, 0)
        total += gates_ref[choice] * pair
        grad_gates_ref[choice] = jnp.sum(cotangent * pair, axis=1, keepdims=True)
        grad_total += dot(place, grads, 0)
    out_ref[...] = total.astype(jnp.bfloat16)
    grad_tokens_ref[...] = grad_total.astype(jnp.bfloat16)
    finish(3)
    arrive(3)
    pick(3)
    weight_grads(False)
    for acc, ref in ((acc_gate, dw_gate_ref), (acc_up, dw_up_ref), (acc_down, dw_down_ref)):
        ref[...] = (acc[...] * (1.0 / REPS)).astype(jnp.bfloat16)
    for step in range(REPS):
        drain(step)
    for which in range(2):
        for shift in range(1, PEERS):
            peer = (e + shift) % PEERS
            back(which, shift, peer, e, peer).wait_send()


def split_bf16(value):
    parts = []
    for _ in range(3):
        top = lax.reduce_precision(value, 8, 7)
        parts.append(top.astype(jnp.bfloat16))
        value = value - top
    return parts


def local_dense(tokens, expert_ids, gate_weights, w_gate, w_up, w_down, grad_out):
    count, width = tokens.shape
    top = expert_ids.shape[1]
    units = w_gate.shape[1]
    share = units // REPS
    capacity = 2 * top * count // PEERS

    chosen = expert_ids[None, :, :] == jnp.arange(PEERS, dtype=jnp.int32)[:, None, None]
    dense_gates = jnp.sum(jnp.where(chosen, gate_weights[None], 0.0), axis=2)
    gate_rows = jnp.stack(split_bf16(dense_gates)).reshape(-1, width)
    gate_rows = jnp.pad(gate_rows, ((0, EXTRA - gate_rows.shape[0]), (0, 0)))
    named = jnp.any(chosen, axis=2).astype(jnp.bfloat16)
    order = jnp.arange(count)
    before = jnp.dot(
        named, (order[:, None] < order[None, :]).astype(jnp.bfloat16), preferred_element_type=jnp.float32
    ).astype(jnp.int32)
    target = expert_ids * capacity + jnp.sum(jnp.where(chosen, before[:, :, None], 0), axis=0)

    dma = pltpu.SemaphoreType.DMA
    vmem = pl.BlockSpec(memory_space=pltpu.VMEM)
    anywhere = pl.BlockSpec(memory_space=pl.ANY)
    bf16, f32 = jnp.bfloat16, jnp.float32
    slots = PEERS * capacity
    out, grad_tokens, grad_gates, *grads = pl.pallas_call(
        moe_kernel,
        out_shape=[
            jax.ShapeDtypeStruct((count, width), bf16),
            jax.ShapeDtypeStruct((count, width), bf16),
            jax.ShapeDtypeStruct((top, count, 1), f32),
            *[jax.ShapeDtypeStruct((share, width), bf16)] * 3,
        ],
        in_specs=[anywhere, anywhere, anywhere, vmem, vmem, anywhere, anywhere, anywhere],
        out_specs=[vmem] * 6,
        scratch_shapes=[
            pltpu.VMEM((REPS, PEERS, 2 * count + EXTRA, width), bf16),
            *[pltpu.VMEM((units, width), bf16)] * 3,
            pltpu.VMEM((slots, width), bf16),
            pltpu.VMEM((slots, width), bf16),
            pltpu.VMEM((PEERS, count), f32),
            pltpu.VMEM((PEERS, count), f32),
            pltpu.VMEM((slots, width), f32),
            pltpu.VMEM((slots, width), f32),
            pltpu.VMEM((2, PEERS, capacity, width), bf16),
            pltpu.VMEM((2, PEERS, capacity, width), bf16),
            *[pltpu.VMEM((share, width), f32)] * 3,
            dma((3,)),
            dma((3,)),
            dma((2,)),
            dma((8, REPS)),
            dma((8, REPS)),
            dma((REPS,)),
            dma((REPS,)),
            dma((REPS,)),
            dma((2, PEERS)),
            dma((2, PEERS)),
        ],
        compiler_params=pltpu.CompilerParams(
            collective_id=0, has_side_effects=True, vmem_limit_bytes=60 * 1024 * 1024
        ),
    )(
        tokens, grad_out, gate_rows, target.T[:, :, None], gate_weights.T[:, :, None],
        w_gate[0], w_up[0], w_down[0],
    )
    return (out, grad_tokens, grad_gates[:, :, 0].T, *[grad[None] for grad in grads])


def solution(mesh):
    in_specs = (
        P(("rep", "exp"), None),
        P(("rep", "exp"), None),
        P(("rep", "exp"), None),
        P("exp", None, None),
        P("exp", None, None),
        P("exp", None, None),
        P(("rep", "exp"), None),
    )
    out_specs = (
        P(("rep", "exp"), None),
        P(("rep", "exp"), None),
        P(("rep", "exp"), None),
        P("exp", "rep", None),
        P("exp", "rep", None),
        P("exp", "rep", None),
    )
    local = local_dense if (mesh.shape["rep"], mesh.shape["exp"]) == (REPS, PEERS) else local_general
    return jax.shard_map(local, mesh=mesh, in_specs=in_specs, out_specs=out_specs, check_vma=False)
```

profile of v0, /device:TPU:0, one launch (start us, length us, event | category | flops | bytes accessed | tf_op | source)
XLA Modules:
  0.0 137.8 jit_solution(11988823001420760248)
XLA Ops:
  0.6 0.7 fusion.5
  1.3 0.1 convolution_convert_fusion
  1.5 0.7 select_reduce_fusion
  2.2 0.7 add_bitcast_fusion
  2.8 0.7 select_reduce_fusion.1
  3.6 0.6 fusion.4.gate_rows_ref
  4.2 0.8 copy.19.target_ref
  5.0 1.5 %copy.20.gates_ref = f32[2,128,1]{2,1,0:T(8,128)} copy(f32[2,128,1]{1,0,2:T(2,128)} %bitcast.23) | data formatting | bytes 2048 | tf_op jit(solution)/shard_map/broadcast_in_dim | solution.py:458
  6.5 122.5 %shard_map.118 = (bf16[128,1024]{1,0:T(8,128)(2,1)}, bf16[128,1024]{1,0:T(8,128)(2,1)}, f32[2,128,1]{2,1,0:T(8,128)}, bf16[352,1024]{1,0:T(8,128)(2,1)}, bf16[35...) custom-call(bf16[128,1024]{1,0:T(8,128)(2,1)} %tokens_ref.1, bf16[128,1024]{1,0:T(8,128)(2,1)} %grads_ref.1, ...), custom_call_target="tpu_custom_call" | custom-call | tf_op jit(solution)/shard_map/pallas_call | solution.py:421
  129.0 0.0 copy-start.1
  129.0 0.0 copy-start
  129.0 1.7 %reduce = f32[2,128]{1,0:T(2,128)} reduce(f32[2,128,1]{2,1,0:T(8,128)} %get-tuple-element.14, f32[]{:T(128)} %constant.15), dimensions={2}, to_apply=%get-tuple-element.14.reduce_sub_computation | reduce | bytes 2052 | tf_op jit(solution)/shard_map/pallas_call | solution.py:421
  130.7 1.7 %copy.26 = bf16[128,1024]{1,0:T(8,128)(2,1)} copy(bf16[128,1024]{1,0:T(8,128)(2,1)} %get-tuple-element.27) | data formatting | bytes 524288
  132.4 1.7 %copy.27 = bf16[128,1024]{1,0:T(8,128)(2,1)} copy(bf16[128,1024]{1,0:T(8,128)(2,1)} %get-tuple-element.28) | data formatting | bytes 524288
  134.0 2.0 %copy.28 = bf16[1,352,1024]{2,1,0:T(8,128)(2,1)} copy(bf16[1,352,1024]{2,1,0:T(8,128)(2,1)} %bitcast.21) | data formatting | bytes 1441792
  136.1 0.0 copy-done.1
  136.1 0.9 copy.29
  136.9 0.0 copy-done
  136.9 0.9 copy.30
  (1 shorter events, 0.0 us)
Async XLA Ops:
  129.0 7.1 %copy-start.1 = (bf16[352,1024]{1,0:T(8,128)(2,1)S(1)}, bf16[352,1024]{1,0:T(8,128)(2,1)}, u32[]{:S(2)}) copy-start(bf16[352,1024]{1,0:T(8,128)(2,1)} %get-tuple-element.16) | copy-start | bytes 2162692
  129.0 7.9 %copy-start = (bf16[352,1024]{1,0:T(8,128)(2,1)S(1)}, bf16[352,1024]{1,0:T(8,128)(2,1)}, u32[]{:S(2)}) copy-start(bf16[352,1024]{1,0:T(8,128)(2,1)} %get-tuple-element.17) | copy-start | bytes 2162692
where the time goes:
time: 139 us; the launch traced here: 138 us
  Pallas kernels  123 us (88%)
  local copies, waits for them, and re-layouts  9.35 us (7%)
  other arithmetic  5.12 us (4%)
    pallas_call x1, Pallas kernels, local_dense(): pl.pallas_call(moe_kernel, out_shape=[jax.ShapeDtypeStruct((count, width)...  123 us
    unnamed x9, local copies, waits for them, and re-layouts  7.07 us

commit v1 on v0

--- a/solution.py
+++ b/solution.py
@@ -96,6 +96,7 @@
 REPS = 4
 PEERS = 8
 EXTRA = 16
+RIDING = 96
 
 
 def dot(a, b, b_dim):
@@ -103,11 +104,12 @@
 
 
 def moe_kernel(
-    tokens_ref, grads_ref, gate_rows_ref, target_ref, gates_ref, w_gate_hbm, w_up_hbm, w_down_hbm,
+    tokens_ref, grads_ref, ids_ref, gates_ref, w_gate_hbm, w_up_hbm, w_down_hbm,
     out_ref, grad_tokens_ref, grad_gates_ref, dw_gate_ref, dw_up_ref, dw_down_ref,
     all_ref, w_gate, w_up, w_down, rows_in, rows_grad, place_ref, gate_ref, out_acc, grad_acc, leaving, returned,
     acc_gate, acc_up, acc_down,
-    load_sem, weight_sem, keep_sem, send_sem, recv_sem, zup_sem, zdown_sem, zrecv_sem, back_send, back_recv,
+    load_sem, weight_sem, keep_sem, send_sem, recv_sem, zup_sem, zdown_sem, zrecv_sem,
+    xup_sem, xdown_sem, xrecv_sem, back_send, back_recv,
 ):
     z = lax.axis_index("rep")
     e = lax.axis_index("exp")
@@ -118,7 +120,9 @@
     rows = all_ref.shape[2]
     capacity = leaving.shape[2]
     share = w_gate.shape[0] // REPS
-    first, second = pl.ds(0, rows // 32 * 16), pl.ds(rows // 32 * 16, rows - rows // 32 * 16)
+    top = ids_ref.shape[1]
+    cut = rows - RIDING
+    riding = pl.ds(cut, RIDING)
 
     side = z // 2
     near = z + side * (3 - 2 * z)
@@ -127,17 +131,43 @@
         mirrored = step - near if step == 1 else step
         layers.append(mirrored + side * (3 - 2 * mirrored))
 
-    mine = all_ref.at[z, e]
     loads = [
         pltpu.make_async_copy(tokens_ref, all_ref.at[z, e, pl.ds(0, count)], load_sem.at[0]),
         pltpu.make_async_copy(grads_ref, all_ref.at[z, e, pl.ds(count, count)], load_sem.at[1]),
-        pltpu.make_async_copy(gate_rows_ref, all_ref.at[z, e, pl.ds(2 * count, EXTRA)], load_sem.at[2]),
     ]
     weights = [
         pltpu.make_async_copy(w_gate_hbm, w_gate, weight_sem.at[0]),
         pltpu.make_async_copy(w_up_hbm, w_up, weight_sem.at[1]),
         pltpu.make_async_copy(w_down_hbm, w_down, weight_sem.at[2]),
     ]
+    def pack_gates():
+        lane = lax.broadcasted_iota(jnp.int32, (count, count), 1)
+        dense = jnp.zeros((count, count), jnp.float32)
+        for choice in range(top):
+            dense += jnp.where(lane == ids_ref[:, choice : choice + 1], gates_ref[:, choice : choice + 1], 0.0)
+        value = dense.T[:PEERS, :]
+        parts = []
+        for _ in range(3):
+            part = value.astype(jnp.bfloat16).astype(jnp.float32)
+            parts.append(part)
+            value = value - part
+        row = lax.broadcasted_iota(jnp.int32, (EXTRA, count), 0)
+        for expert in range(PEERS):
+            tile = jnp.zeros((EXTRA, count), jnp.float32)
+            for index, part in enumerate(parts):
+                tile = jnp.where(row == index, part[expert : expert + 1, :], tile)
+            lanes = pl.ds(expert * count, count)
+            all_ref[z, e, pl.ds(2 * count, EXTRA), lanes] = tile.astype(jnp.bfloat16)
+
+    def targets():
+        lane = lax.broadcasted_iota(jnp.int32, (count, count), 1)
+        row = lax.broadcasted_iota(jnp.int32, (count, count), 0)
+        picks = [lane == ids_ref[:, choice : choice + 1] for choice in range(top)]
+        named = sum(jnp.where(picked, 1.0, 0.0) for picked in picks)
+        before = dot(jnp.where(lane < row, 1.0, 0.0).astype(jnp.bfloat16), named.astype(jnp.bfloat16), 0)
+        slot = before + (lane * capacity).astype(jnp.float32)
+        return [jnp.sum(jnp.where(picked, slot, 0.0), axis=1, keepdims=True) for picked in picks]
+
     for copy in loads:
         copy.start()
     for copy in weights:
@@ -156,6 +186,7 @@
     def _():
         pl.semaphore_signal(barrier, inc=1, device_id={"rep": z + 1, "exp": e}, device_id_type=MESH)
 
+    pack_gates()
     inside = jnp.logical_and(z > 0, z < REPS - 1)
 
     @pl.when(inside)
@@ -187,10 +218,17 @@
             device_id_type=MESH,
         )
 
-    def direct(layer):
-        return [plane(0, layer, e, None, xn), plane(1, layer, e, None, yn), plane(2, layer, e, None, sib)]
-
-    def relayed(layer):
+    def spans(step):
+        whole = rows if step == 0 else cut
+        half = whole // 32 * 16
+        return pl.ds(0, whole), pl.ds(0, half), pl.ds(half, whole - half)
+
+    def direct(step):
+        layer, (whole, _, _) = layers[step], spans(step)
+        return [plane(0, layer, e, whole, xn), plane(1, layer, e, whole, yn), plane(2, layer, e, None, sib)]
+
+    def relayed(step):
+        layer, (_, first, second) = layers[step], spans(step)
         return [
             plane(3, layer, xn, first, yn),
             plane(5, layer, xn, None, sib),
@@ -207,28 +245,57 @@
         def _():
             action(along(zdown_sem, layer, -1))
 
+    def rider(sem, index, layer, step):
+        block = all_ref.at[layer, (xn, yn, diag)[index], riding]
+        return pltpu.make_async_remote_copy(
+            src_ref=block,
+            dst_ref=block,
+            send_sem=sem.at[index, layer],
+            recv_sem=xrecv_sem.at[index, layer],
+            device_id={"rep": z + step, "exp": e},
+            device_id_type=MESH,
+        )
+
+    def pass_rider(index, layer, action):
+        @pl.when(jnp.logical_and(layer <= z, z < REPS - 1))
+        def _():
+            action(rider(xup_sem, index, layer, 1))
+
+        @pl.when(jnp.logical_and(layer >= z, z > 0))
+        def _():
+            action(rider(xdown_sem, index, layer, -1))
+
+    def ride(step, index):
+        layer = layers[step]
+        if step:
+            rider(xup_sem, index, layer, 0).wait_recv()
+        pass_rider(index, layer, lambda copy: copy.start())
+
     def inject(step):
         layer = layers[step]
         if step:
             along(zup_sem, layer, 0).wait_recv()
         pass_on(layer, lambda copy: copy.start())
-        for copy in direct(layer):
+        for copy in direct(step):
             copy.start()
 
     def forward(step):
-        layer = layers[step]
-        copies = relayed(layer)
-        plane(0, layer, xn, None, xn).wait_recv()
+        layer, (whole, _, _) = layers[step], spans(step)
+        copies = relayed(step)
+        plane(0, layer, xn, whole, xn).wait_recv()
         copies[0].start()
+        plane(1, layer, yn, whole, yn).wait_recv()
+        copies[2].start()
+        ride(step, 0)
         copies[1].start()
-        plane(1, layer, yn, None, yn).wait_recv()
-        copies[2].start()
+        ride(step, 1)
         copies[3].start()
 
     def finish(step):
-        layer = layers[step]
+        layer, (_, first, second) = layers[step], spans(step)
         plane(3, layer, diag, first, yn).wait_recv()
         plane(4, layer, diag, second, xn).wait_recv()
+        ride(step, 2)
         plane(7, layer, diag, None, sib).start()
 
     def arrive(step):
@@ -237,9 +304,11 @@
 
     def drain(step):
         layer = layers[step]
-        for copy in direct(layer) + relayed(layer) + [plane(7, layer, diag, None, sib)]:
+        for copy in direct(step) + relayed(step) + [plane(7, layer, diag, None, sib)]:
             copy.wait_send()
         pass_on(layer, lambda copy: copy.wait_send())
+        for index in range(3):
+            pass_rider(index, layer, lambda copy: copy.wait_send())
 
     def pick(step):
         layer = layers[step]
@@ -360,15 +429,16 @@
             back(which, shift, source, source, source).wait_recv()
     outputs = returned[0].reshape(PEERS * capacity, width)
     grads = returned[1].reshape(PEERS * capacity, width)
-    column = lax.broadcasted_iota(jnp.int32, (count, PEERS * capacity), 1)
+    column = lax.broadcasted_iota(jnp.int32, (count, PEERS * capacity), 1).astype(jnp.float32)
+    target = targets()
     total = jnp.zeros((count, width), jnp.float32)
     grad_total = jnp.zeros((count, width), jnp.float32)
     cotangent = all_ref[z, e, pl.ds(count, count), :].astype(jnp.float32)
-    for choice in range(target_ref.shape[0]):
-        place = jnp.where(column == target_ref[choice], 1.0, 0.0).astype(jnp.bfloat16)
+    for choice in range(top):
+        place = jnp.where(column == target[choice], 1.0, 0.0).astype(jnp.bfloat16)
         pair = dot(place, outputs, 0)
-        total += gates_ref[choice] * pair
-        grad_gates_ref[choice] = jnp.sum(cotangent * pair, axis=1, keepdims=True)
+        total += gates_ref[:, choice : choice + 1] * pair
+        grad_gates_ref[:, choice : choice + 1] = jnp.sum(cotangent * pair, axis=1, keepdims=True)
         grad_total += dot(place, grads, 0)
     out_ref[...] = total.astype(jnp.bfloat16)
     grad_tokens_ref[...] = grad_total.astype(jnp.bfloat16)
@@ -386,13 +456,13 @@
             back(which, shift, peer, e, peer).wait_send()
 
 
-def split_bf16(value):
-    parts = []
-    for _ in range(3):
-        top = lax.reduce_precision(value, 8, 7)
-        parts.append(top.astype(jnp.bfloat16))
-        value = value - top
-    return parts
+def store_kernel(*refs):
+    half = len(refs) // 2
+    copies = [pltpu.make_async_copy(refs[i], refs[half + i], refs[-1].at[i]) for i in range(half)]
+    for copy in copies:
+        copy.start()
+    for copy in copies:
+        copy.wait()
 
 
 def local_dense(tokens, expert_ids, gate_weights, w_gate, w_up, w_down, grad_out):
@@ -402,31 +472,20 @@
     share = units // REPS
     capacity = 2 * top * count // PEERS
 
-    chosen = expert_ids[None, :, :] == jnp.arange(PEERS, dtype=jnp.int32)[:, None, None]
-    dense_gates = jnp.sum(jnp.where(chosen, gate_weights[None], 0.0), axis=2)
-    gate_rows = jnp.stack(split_bf16(dense_gates)).reshape(-1, width)
-    gate_rows = jnp.pad(gate_rows, ((0, EXTRA - gate_rows.shape[0]), (0, 0)))
-    named = jnp.any(chosen, axis=2).astype(jnp.bfloat16)
-    order = jnp.arange(count)
-    before = jnp.dot(
-        named, (order[:, None] < order[None, :]).astype(jnp.bfloat16), preferred_element_type=jnp.float32
-    ).astype(jnp.int32)
-    target = expert_ids * capacity + jnp.sum(jnp.where(chosen, before[:, :, None], 0), axis=0)
-
     dma = pltpu.SemaphoreType.DMA
     vmem = pl.BlockSpec(memory_space=pltpu.VMEM)
     anywhere = pl.BlockSpec(memory_space=pl.ANY)
     bf16, f32 = jnp.bfloat16, jnp.float32
     slots = PEERS * capacity
-    out, grad_tokens, grad_gates, *grads = pl.pallas_call(
+    results = pl.pallas_call(
         moe_kernel,
         out_shape=[
             jax.ShapeDtypeStruct((count, width), bf16),
             jax.ShapeDtypeStruct((count, width), bf16),
-            jax.ShapeDtypeStruct((top, count, 1), f32),
+            jax.ShapeDtypeStruct((count, top), f32),
             *[jax.ShapeDtypeStruct((share, width), bf16)] * 3,
         ],
-        in_specs=[anywhere, anywhere, anywhere, vmem, vmem, anywhere, anywhere, anywhere],
+        in_specs=[anywhere, anywhere, vmem, vmem, anywhere, anywhere, anywhere],
         out_specs=[vmem] * 6,
         scratch_shapes=[
             pltpu.VMEM((REPS, PEERS, 2 * count + EXTRA, width), bf16),
@@ -440,7 +499,7 @@
             pltpu.VMEM((2, PEERS, capacity, width), bf16),
             pltpu.VMEM((2, PEERS, capacity, width), bf16),
             *[pltpu.VMEM((share, width), f32)] * 3,
-            dma((3,)),
+            dma((2,)),
             dma((3,)),
             dma((2,)),
             dma((8, REPS)),
@@ -448,6 +507,9 @@
             dma((REPS,)),
             dma((REPS,)),
             dma((REPS,)),
+            dma((3, REPS)),
+            dma((3, REPS)),
+            dma((3, REPS)),
             dma((2, PEERS)),
             dma((2, PEERS)),
         ],
@@ -455,10 +517,16 @@
             collective_id=0, has_side_effects=True, vmem_limit_bytes=60 * 1024 * 1024
         ),
     )(
-        tokens, grad_out, gate_rows, target.T[:, :, None], gate_weights.T[:, :, None],
-        w_gate[0], w_up[0], w_down[0],
+        tokens, grad_out, expert_ids, gate_weights, w_gate[0], w_up[0], w_down[0],
     )
-    return (out, grad_tokens, grad_gates[:, :, 0].T, *[grad[None] for grad in grads])
+    out, grad_tokens, grad_gates, *grads = pl.pallas_call(
+        store_kernel,
+        out_shape=[jax.ShapeDtypeStruct(result.shape, result.dtype) for result in results],
+        in_specs=[anywhere] * len(results),
+        out_specs=[anywhere] * len(results),
+        scratch_shapes=[dma((len(results),))],
+    )(*results)
+    return (out, grad_tokens, grad_gates, *[grad[None] for grad in grads])
 
 
 def solution(mesh):

time: 139 us -> 203 us (1.46)
  Pallas kernels: 123 us -> 196 us
  other arithmetic: 5.12 us -> 0 us
  local copies, waits for them, and re-layouts: 9.35 us -> 4.3 us
    pallas_call x0 -> x1, Pallas kernels: none -> 84.5 us  [local_dense(): pl.pallas_call(store_kernel, out_shape=[jax.ShapeDtypeStruct(result.shape...]
    pallas_call x1, Pallas kernels: 123 us -> 112 us  [local_dense(): pl.pallas_call(moe_kernel, out_shape=[jax.ShapeDtypeStruct((count, width)...]
    unnamed x9 -> x3, local copies, waits for them, and re-layouts: 7.07 us -> 4.3 us
    broadcast_in_dim x2 -> x0, local copies, waits for them, and re-layouts: 2.27 us -> none  [the longest x1 1.47 us: local_dense(): gate_weights.T[:, :, None]]
where the time goes in v1:
time: 203 us; the launch traced here: 201 us
  Pallas kernels  196 us (97%)
  local copies, waits for them, and re-layouts  4.3 us (2%)
    pallas_call x1, Pallas kernels, local_dense(): pl.pallas_call(moe_kernel, out_shape=[jax.ShapeDtypeStruct((count, width)...  112 us
    pallas_call x1, Pallas kernels, local_dense(): pl.pallas_call(store_kernel, out_shape=[jax.ShapeDtypeStruct(result.shape...  84.5 us
    unnamed x3, local copies, waits for them, and re-layouts  4.3 us

profile of v1, /device:TPU:0, one launch (start us, length us, event | category | flops | bytes accessed | tf_op | source)
XLA Modules:
  0.0 201.3 jit_solution(4553466901007404789)
XLA Ops:
  0.6 1.4 copy.13.ids_ref
  2.0 1.4 copy.14.gates_ref
  3.5 111.9 %shard_map.118 = (bf16[128,1024]{1,0:T(8,128)(2,1)}, bf16[128,1024]{1,0:T(8,128)(2,1)}, f32[128,2]{1,0:T(8,128)}, bf16[352,1024]{1,0:T(8,128)(2,1)}, bf16[352,10...) custom-call(bf16[128,1024]{1,0:T(8,128)(2,1)} %tokens_ref.1, bf16[128,1024]{1,0:T(8,128)(2,1)} %grads_ref.1, ...), custom_call_target="tpu_custom_call" | custom-call | tf_op jit(solution)/shard_map/pallas_call | solution.py:480
  115.3 84.5 %shard_map.119 = (bf16[128,1024]{1,0:T(8,128)(2,1)}, bf16[128,1024]{1,0:T(8,128)(2,1)}, f32[128,2]{1,0:T(8,128)}, bf16[352,1024]{1,0:T(8,128)(2,1)}, bf16[352,10...) custom-call(bf16[128,1024]{1,0:T(8,128)(2,1)} %get-tuple-element.18.refs_0_, bf16[128,1024]{1,0:T(8,128)(2,1)} %get-tuple-element.19.refs_1_, ...), custom_call_target="tpu_custom_call" | custom-call | tf_op jit(solution)/shard_map/pallas_call | solution.py:522
  199.9 1.5 copy.15

commit v2 on v1

--- a/solution.py
+++ b/solution.py
@@ -120,7 +120,7 @@
     rows = all_ref.shape[2]
     capacity = leaving.shape[2]
     share = w_gate.shape[0] // REPS
-    top = ids_ref.shape[1]
+    top = ids_ref.shape[0]
     cut = rows - RIDING
     riding = pl.ds(cut, RIDING)
 
@@ -141,11 +141,10 @@
         pltpu.make_async_copy(w_down_hbm, w_down, weight_sem.at[2]),
     ]
     def pack_gates():
-        lane = lax.broadcasted_iota(jnp.int32, (count, count), 1)
-        dense = jnp.zeros((count, count), jnp.float32)
+        line = lax.broadcasted_iota(jnp.int32, (PEERS, count), 0)
+        value = jnp.zeros((PEERS, count), jnp.float32)
         for choice in range(top):
-            dense += jnp.where(lane == ids_ref[:, choice : choice + 1], gates_ref[:, choice : choice + 1], 0.0)
-        value = dense.T[:PEERS, :]
+            value += jnp.where(line == ids_ref[choice : choice + 1, :], gates_ref[choice : choice + 1, :], 0.0)
         parts = []
         for _ in range(3):
             part = value.astype(jnp.bfloat16).astype(jnp.float32)
@@ -159,14 +158,20 @@
             lanes = pl.ds(expert * count, count)
             all_ref[z, e, pl.ds(2 * count, EXTRA), lanes] = tile.astype(jnp.bfloat16)
 
-    def targets():
+    def pair_columns():
+        line = lax.broadcasted_iota(jnp.int32, (PEERS, count), 0)
+        picks = [line == ids_ref[choice : choice + 1, :] for choice in range(top)]
+        named = sum(jnp.where(picked, 1.0, 0.0) for picked in picks)
+        row = lax.broadcasted_iota(jnp.int32, (count, count), 0)
         lane = lax.broadcasted_iota(jnp.int32, (count, count), 1)
-        row = lax.broadcasted_iota(jnp.int32, (count, count), 0)
-        picks = [lane == ids_ref[:, choice : choice + 1] for choice in range(top)]
-        named = sum(jnp.where(picked, 1.0, 0.0) for picked in picks)
-        before = dot(jnp.where(lane < row, 1.0, 0.0).astype(jnp.bfloat16), named.astype(jnp.bfloat16), 0)
-        slot = before + (lane * capacity).astype(jnp.float32)
-        return [jnp.sum(jnp.where(picked, slot, 0.0), axis=1, keepdims=True) for picked in picks]
+        before = dot(named.astype(jnp.bfloat16), jnp.where(row < lane, 1.0, 0.0).astype(jnp.bfloat16), 0)
+        slot = before + (line * capacity).astype(jnp.float32)
+        table = jnp.zeros((count, count), jnp.float32)
+        for choice, picked in enumerate(picks):
+            target = jnp.sum(jnp.where(picked, slot, 0.0), axis=0, keepdims=True)
+            table = jnp.where(row == choice, target, table)
+            table = jnp.where(row == top + choice, gates_ref[choice : choice + 1, :], table)
+        return table.T
 
     for copy in loads:
         copy.start()
@@ -430,16 +435,19 @@
     outputs = returned[0].reshape(PEERS * capacity, width)
     grads = returned[1].reshape(PEERS * capacity, width)
     column = lax.broadcasted_iota(jnp.int32, (count, PEERS * capacity), 1).astype(jnp.float32)
-    target = targets()
+    columns = pair_columns()
+    lane = lax.broadcasted_iota(jnp.int32, (count, count), 1)
+    table = jnp.zeros((count, count), jnp.float32)
     total = jnp.zeros((count, width), jnp.float32)
     grad_total = jnp.zeros((count, width), jnp.float32)
     cotangent = all_ref[z, e, pl.ds(count, count), :].astype(jnp.float32)
     for choice in range(top):
-        place = jnp.where(column == target[choice], 1.0, 0.0).astype(jnp.bfloat16)
+        place = jnp.where(column == columns[:, choice : choice + 1], 1.0, 0.0).astype(jnp.bfloat16)
         pair = dot(place, outputs, 0)
-        total += gates_ref[:, choice : choice + 1] * pair
-        grad_gates_ref[:, choice : choice + 1] = jnp.sum(cotangent * pair, axis=1, keepdims=True)
+        total += columns[:, top + choice : top + choice + 1] * pair
+        table = jnp.where(lane == choice, jnp.sum(cotangent * pair, axis=1, keepdims=True), table)
         grad_total += dot(place, grads, 0)
+    grad_gates_ref[...] = table.T[:top, :]
     out_ref[...] = total.astype(jnp.bfloat16)
     grad_tokens_ref[...] = grad_total.astype(jnp.bfloat16)
     finish(3)
@@ -482,7 +490,7 @@
         out_shape=[
             jax.ShapeDtypeStruct((count, width), bf16),
             jax.ShapeDtypeStruct((count, width), bf16),
-            jax.ShapeDtypeStruct((count, top), f32),
+            jax.ShapeDtypeStruct((top, count), f32),
             *[jax.ShapeDtypeStruct((share, width), bf16)] * 3,
         ],
         in_specs=[anywhere, anywhere, vmem, vmem, anywhere, anywhere, anywhere],
@@ -517,16 +525,16 @@
             collective_id=0, has_side_effects=True, vmem_limit_bytes=60 * 1024 * 1024
         ),
     )(
-        tokens, grad_out, expert_ids, gate_weights, w_gate[0], w_up[0], w_down[0],
+        tokens, grad_out, expert_ids.T, gate_weights.T, w_gate[0], w_up[0], w_down[0],
     )
     out, grad_tokens, grad_gates, *grads = pl.pallas_call(
         store_kernel,
         out_shape=[jax.ShapeDtypeStruct(result.shape, result.dtype) for result in results],
-        in_specs=[anywhere] * len(results),
+        in_specs=[vmem] * len(results),
         out_specs=[anywhere] * len(results),
         scratch_shapes=[dma((len(results),))],
     )(*results)
-    return (out, grad_tokens, grad_gates, *[grad[None] for grad in grads])
+    return (out, grad_tokens, grad_gates.T, *[grad[None] for grad in grads])
 
 
 def solution(mesh):

time: 203 us -> 117 us (0.58)
  Pallas kernels: 196 us -> 115 us
  local copies, waits for them, and re-layouts: 4.3 us -> 0 us
    pallas_call x1, Pallas kernels: 84.5 us -> 3.27 us  [local_dense(): pl.pallas_call(store_kernel, out_shape=[jax.ShapeDtypeStruct(result.shape...]
    unnamed x3 -> x0, local copies, waits for them, and re-layouts: 4.3 us -> none
where the time goes in v2:
time: 117 us; the launch traced here: 116 us
  Pallas kernels  115 us (98%)
    pallas_call x1, Pallas kernels, local_dense(): pl.pallas_call(moe_kernel, out_shape=[jax.ShapeDtypeStruct((count, width)...  112 us
    pallas_call x1, Pallas kernels, local_dense(): pl.pallas_call(store_kernel, out_shape=[jax.ShapeDtypeStruct(result.shape...  3.27 us

profile of v2, /device:TPU:0, one launch (start us, length us, event | category | flops | bytes accessed | tf_op | source)
XLA Modules:
  0.0 115.8 jit_solution(9211403584450303869)
XLA Ops:
  0.6 111.7 %shard_map.118 = (bf16[128,1024]{1,0:T(8,128)(2,1)}, bf16[128,1024]{1,0:T(8,128)(2,1)}, f32[2,128]{1,0:T(2,128)}, bf16[352,1024]{1,0:T(8,128)(2,1)}, bf16[352,10...) custom-call(bf16[128,1024]{1,0:T(8,128)(2,1)} %tokens_ref.1, bf16[128,1024]{1,0:T(8,128)(2,1)} %grads_ref.1, s32[2,128]{1,0:T(2,128)} %bitcast.12, ...), custom_call_target="tpu_custom_call" | custom-call | tf_op jit(solution)/shard_map/pallas_call | solution.py:488
  112.4 3.3 %shard_map.119 = (bf16[128,1024]{1,0:T(8,128)(2,1)}, bf16[128,1024]{1,0:T(8,128)(2,1)}, f32[2,128]{1,0:T(2,128)}, bf16[352,1024]{1,0:T(8,128)(2,1)}, bf16[352,10...) custom-call(bf16[128,1024]{1,0:T(8,128)(2,1)} %get-tuple-element.18.refs_0_, bf16[128,1024]{1,0:T(8,128)(2,1)} %get-tuple-element.19.refs_1_, ...), custom_call_target="tpu_custom_call" | custom-call | tf_op jit(solution)/shard_map/pallas_call | solution.py:530
